TPU v7x, 256 devices: a whole 4x4x8 slice. The times are simulated.
256 devices in a mesh: grp: 16 (over y, x), seq: 16 (over z, core).
Axes of the slice: x: 4, y: 4, z: 8, core: 2. Of those that a mesh axis runs over, the one named last changes fastest.
Arguments:
- audio: bfloat16 [16, 4096, 1280], P('grp', 'seq'), may hold values from -6 to 6, as said below
- block_ids: int32 [16, 4096], P('grp', 'seq'), may hold values from 0 to 80, never falling along the last dimension, each value on 1 to 100 neighbouring positions
- norm_gain: float32 [1280], replicated, may hold values from 0.1 to 1.9
- qkv_weight: bfloat16 [1280, 3840], P(None, 'grp'), may hold values from -8 to 8
- out_weight: bfloat16 [1280, 1280], P(None, 'grp'), may hold values from -0.15625 to 0.15625
- adapter_weight: bfloat16 [2560, 2048], P(None, 'grp'), may hold values from -0.125 to 0.125
- moe_gain: float32 [2048], replicated, may hold values from 0.1 to 1.9
- gate_weight: bfloat16 [16, 2048, 768], P('seq'), may hold values from -0.125 to 0.125
- up_weight: bfloat16 [16, 2048, 768], P('seq'), may hold values from -0.125 to 0.125
- down_weight: bfloat16 [16, 768, 2048], P('seq'), may hold values from -0.21875 to 0.21875
- routes: int32 [16, 2048, 4], P('grp', 'seq'), may hold values from 0 to 15, all different within a row; in each aligned block of 128 rows (0 to 127, 128 to 255, ..., all dimensions but the last counted through in order) at most 48 rows name the same one
- route_weights: float32 [16, 2048, 4], P('grp', 'seq'), may hold values from 0.05 to 1
Outputs:
- thinker_out: bfloat16 [16, 2048, 2048], P('grp', 'seq')
Inputs may be any that keep to these rules, and one draw needn't show every extreme that they name: `audio`: in the hidden draw, frames come in nearly equal adjacent pairs. `block_ids`: block numbers never fall along a slab's frames; each block holds 1 to 100 frames, and some block exactly 100. `routes`: each token names 4 different experts; among the tokens of one device no expert is named by more than 48 of them, and in every draw some expert is named by exactly 48.
All inputs are finite; a program needn't handle non-finite values.
Results may differ from a plain program's by a relative error of at most 0.011.
Values may be sent and summed in bfloat16 or wider, within the bound.
No kernel may reach another device: no remote copies, remote signals or barrier semaphores. Data moves between devices by JAX's collectives and lax.ppermute only.
A program may use at most 128 MiB of HBM per device.

v0:
```python
import jax
import jax.numpy as jnp
from jax import lax
from jax.sharding import Mesh
from jax.sharding import PartitionSpec as P

HEADS = 20
HEAD = 64
WIN = 100
GRP = ("grp_0", "grp_1")
LN_EPSILON = 1e-05
RMS_EPSILON = 1e-06
MASKED = -1e30


def extended(cells, sides, width):
    for axis, dim in sides:
        count = lax.axis_size(axis)
        ends = count - 1
        head = lax.slice_in_dim(cells, 0, width, axis=dim)
        tail = lax.slice_in_dim(cells, cells.shape[dim] - width, cells.shape[dim], axis=dim)
        cells = jnp.concatenate(
            [
                lax.ppermute(tail, axis, [(i, (i + 1) % count) for i in range(ends)]),
                cells,
                lax.ppermute(head, axis, [((i + 1) % count, i) for i in range(ends)]),
            ],
            axis=dim,
        )
    return cells


def gather_axes(value, axes, dim):
    out = value
    for number in range(len(axes) - 1, -1, -1):
        out = lax.all_gather(out, axes[number], axis=dim, tiled=True)
    return out


def layer_norm(signal, gain):
    widened = signal.astype(jnp.float32)
    average = jnp.mean(widened, axis=-1, keepdims=True)
    centred = widened - average
    variance = jnp.mean(centred * centred, axis=-1, keepdims=True)
    return centred * lax.rsqrt(variance + LN_EPSILON) * gain


def rms_norm(signal, gain):
    widened = signal.astype(jnp.float32)
    squares = jnp.mean(widened * widened, axis=-1, keepdims=True)
    return widened * lax.rsqrt(squares + RMS_EPSILON) * gain


def body(
    audio,
    block_ids,
    norm_gain,
    qkv_weight,
    out_weight,
    adapter_weight,
    moe_gain,
    gate_weight,
    up_weight,
    down_weight,
    routes,
    route_weights,
):
    frames = audio.shape[1]
    width = audio.shape[2]
    margin = WIN - 1
    signal = audio[0]
    normed = layer_norm(signal, norm_gain).astype(jnp.bfloat16)
    qkv_all = jnp.dot(
        normed,
        lax.all_gather(qkv_weight, GRP, axis=1, tiled=True),
        preferred_element_type=jnp.float32,
    ).astype(jnp.bfloat16)
    tags = (block_ids[0] % 256 + 1).astype(jnp.float32).astype(jnp.bfloat16)
    key_value = qkv_all[:, width:]
    padded_pairs, padded_tags = (
        extended(key_value, (("seq", 0),), margin),
        extended(tags, (("seq", 0),), margin),
    )
    query_rows = qkv_all[:, :width].reshape(frames, HEADS, HEAD)
    key_rows = padded_pairs[:, :width].reshape(-1, HEADS, HEAD)
    value_rows = padded_pairs[:, width:].reshape(-1, HEADS, HEAD)
    scores = jnp.einsum(
        "qhd,khd->hqk", query_rows, key_rows, preferred_element_type=jnp.float32
    ) * HEAD ** (-0.5)
    query_tags = tags.astype(jnp.float32)
    key_tags = padded_tags.astype(jnp.float32)
    distance = (
        jnp.arange(frames, dtype=jnp.int32)[:, None]
        + margin
        - jnp.arange(frames + 2 * margin, dtype=jnp.int32)[None, :]
    )
    allowed = (query_tags[:, None] == key_tags[None, :]) & (jnp.abs(distance) < WIN)
    scores = jnp.where(allowed[None], scores, MASKED)
    highest = jnp.max(scores, axis=-1, keepdims=True)
    exponent = jnp.exp(scores - highest)
    probability = (exponent / jnp.sum(exponent, axis=-1, keepdims=True)).astype(jnp.bfloat16)
    attended = jnp.einsum(
        "hqk,khd->qhd", probability, value_rows, preferred_element_type=jnp.float32
    )
    attended = attended.astype(jnp.bfloat16).reshape(frames, width)
    projected = jnp.dot(
        attended, gather_axes(out_weight, GRP, 1), preferred_element_type=jnp.float32
    )
    encoded = (signal.astype(jnp.float32) + projected).astype(jnp.bfloat16)
    pooled = encoded.reshape(frames // 2, 2 * width)
    thinker_in = jnp.dot(
        pooled,
        lax.all_gather(adapter_weight, GRP, axis=1, tiled=True),
        preferred_element_type=jnp.float32,
    ).astype(jnp.bfloat16)
    expert_in = rms_norm(thinker_in, moe_gain).astype(jnp.bfloat16)
    local_experts = gate_weight.shape[0]
    experts_total = local_experts * lax.axis_size("seq")
    picked_routes = routes[0]
    tokens_here, route_count = picked_routes.shape
    capacity = 3 * tokens_here * route_count // (2 * experts_total)
    chosen_experts = picked_routes.reshape(-1)
    expert_ids = jnp.arange(experts_total, dtype=jnp.int32)
    membership = (chosen_experts[:, None] == expert_ids[None, :]).astype(jnp.int32)
    positions = jnp.sum((jnp.cumsum(membership, axis=0) - 1) * membership, axis=1)
    slot_index = chosen_experts * capacity + positions
    slot_grid = slot_index.reshape(tokens_here, route_count)
    slot_ids = jnp.arange(experts_total * capacity, dtype=jnp.int32)
    dispatch_matrix = jnp.any(slot_grid[None, :, :] == slot_ids[:, None, None], axis=2).astype(
        jnp.bfloat16
    )
    outgoing = jnp.dot(dispatch_matrix, expert_in, preferred_element_type=jnp.float32).astype(
        jnp.bfloat16
    )
    outgoing = outgoing.reshape(experts_total, capacity, expert_in.shape[1])
    arrived = lax.all_to_all(outgoing, "seq", split_axis=0, concat_axis=0, tiled=True)
    senders = arrived.shape[0] // local_experts
    grouped = arrived.reshape(senders, local_experts, arrived.shape[1], arrived.shape[2])
    gate_act = jnp.einsum(
        "secd,edf->secf", grouped, gate_weight, preferred_element_type=jnp.float32
    )
    up_act = jnp.einsum("secd,edf->secf", grouped, up_weight, preferred_element_type=jnp.float32)
    hidden = (jax.nn.silu(gate_act) * up_act).astype(jnp.bfloat16)
    produced = jnp.einsum("secf,efd->secd", hidden, down_weight, preferred_element_type=jnp.float32)
    produced = produced.astype(jnp.bfloat16).reshape(arrived.shape)
    returned = lax.all_to_all(produced, "seq", split_axis=0, concat_axis=0, tiled=True)
    flat_returned = returned.reshape(experts_total * capacity, returned.shape[2])
    picked_rows = (
        flat_returned[slot_index].astype(jnp.float32).reshape(tokens_here, route_count, -1)
    )
    weights_here = route_weights[0]
    shares = weights_here / jnp.sum(weights_here, axis=1, keepdims=True)
    combined = jnp.sum(shares[:, :, None] * picked_rows, axis=1)
    thinker_out = (thinker_in.astype(jnp.float32) + combined).astype(jnp.bfloat16)
    return thinker_out[None]


def solution(mesh):
    torus = Mesh(mesh.devices.reshape(4, 4, mesh.shape["seq"]), ("grp_0", "grp_1", "seq"))
    in_specs = (
        P(GRP, "seq", None),
        P(GRP, "seq"),
        P(),
        P(None, GRP),
        P(None, GRP),
        P(None, GRP),
        P(),
        P("seq", None, None),
        P("seq", None, None),
        P("seq", None, None),
        P(GRP, "seq", None),
        P(GRP, "seq", None),
    )
    out_specs = P(GRP, "seq", None)
    return jax.shard_map(body, mesh=torus, in_specs=in_specs, out_specs=out_specs, check_vma=False)
```

profile of v0, /device:TPU:1, one launch (start us, length us, event | category | flops | bytes accessed | tf_op | source)
XLA Modules:
  0.0 440.4 jit_solution(11311125937926482085)
XLA Ops:
  6.5 0.7 all-gather.4.cloned.1.call-update
  7.3 0.0 all-gather.6.cloned.1.call-start
  7.3 14.3 %all_gather.13 = bf16[1280,320]{0,1:T(8,128)(2,1)} all-gather(bf16[1280,80]{0,1:T(8,128)(2,1)} %param.16), channel_id=1, replica_groups=mesh['grp_0'=4,'grp_1'=4,'seq'=16] {'grp_1'}, dimensions={1}, use_global_device_ids=true | all-gather | bytes 1024000 | tf_op jit(solution)/shard_map/all_gather | solution.py:36
  21.6 0.0 all-gather.6.cloned.1.call-update
  21.7 0.0 all-gather.8.cloned.1.call-start
  21.7 0.7 all-gather.8.cloned.1.call-update
  22.4 0.7 fusion.57
  23.1 0.1 fusion.61
  23.2 6.9 %collective-permute-start.2 = (bf16[99]{0:T(256)(128)(2,1)S(1)}, bf16[99]{0:T(256)(128)(2,1)S(1)}, u32[]{:S(2)}, u32[]{:S(2)}) collective-permute-start(bf16[99]{0:T(256)(128)(2,1)S(1)} %get-tuple-element.13), channel_id=1, source_target_pairs={{0,1},{1,2},{2,3},{3,4},{4,5},{5,6},{6,7},{7,8},{8,9},{9,10},{10,1... | collective-permute-start | bytes 602 | tf_op jit(solution)/shard_map/ppermute | solution.py:24
  30.1 1.9 collective-permute-start.3
  32.0 0.8 copy.30
  32.8 0.1 eq.66
  32.9 0.1 eq.62
  33.0 1.2 reduce-window.6
  34.2 0.2 slice_reduce_fusion
  34.4 0.1 fusion.43
  34.5 0.1 reduce_sum.72
  34.7 0.1 copy.34
  34.7 0.2 fusion.20
  35.0 1.3 convert_reduce_fusion
  36.3 1.4 fusion.27
  37.7 0.0 copy-start.6
  37.7 58.1 %all-gather.4.cloned.1.call-done = bf16[1280,3840]{0,1:T(8,128)(2,1)} async-done(((bf16[1280,240]{0,1:T(8,128)(2,1)}), bf16[1280,3840]{0,1:T(8,128)(2,1)}) %all-gather.4.cloned.1.call-update) | async-done | bytes 9830416 | tf_op jit(solution)/shard_map/all_gather | solution.py:75
  95.8 0.0 copy-done.8
  95.8 6.8 %convolution_convert_fusion = bf16[256,3840]{1,0:T(8,128)(2,1)S(1)} fusion(bf16[1280,3840]{0,1:T(8,128)(2,1)} %all-gather.4.cloned.1.call-done, bf16[1,256,1280]{2,1,0:T(8,128)(2,1)} %param.12, f32[1280]{0:T(1024)S(1)} %copy-done.8, f32[256]{0:T(256)S(1)} %add_rsqrt_fusion, f32[256]{0:T(256)S(1)} %broadcast_multiply_fusion.1), kind=kOutput, calls=%fused_computation.6 | convolution fusion | flops 2519203840 | bytes 12459008 | tf_op jit(solution)/shard_map/dot_general | solution.py:73
  102.6 1.1 fusion.60
  103.7 3.9 collective-permute-start
  107.6 2.1 collective-permute-start.1
  109.8 0.0 collective-permute-done.2
  109.8 0.0 collective-permute-done.3
  109.8 0.1 maximum_convert_fusion
  109.9 0.2 fusion.41
  110.1 1.2 slice.45
  111.3 0.9 slice.48
  112.1 2.2 copy.27
  114.3 0.0 collective-permute-done
  114.3 4.5 %collective-permute-done.1 = bf16[99,2560]{1,0:T(8,128)(2,1)} collective-permute-done((bf16[99,2560]{1,0:T(8,128)(2,1)}, bf16[99,2560]{1,0:T(8,128)(2,1)}, u32[]{:S(2)}, u32[]{:S(2)}) %collective-permute-start.1) | collective-permute-done | bytes 506912 | tf_op jit(solution)/shard_map/ppermute | solution.py:26
  118.8 2.1 pad_maximum_fusion
  120.9 1.6 fusion.59
  122.5 2.4 copy.28
  124.9 2.4 copy.26
  127.4 8.2 %fusion.62 = (f32[20,256]{1,0:T(8,128)S(1)}, f32[20,256,454]{1,2,0:T(8,128)}) fusion(pred[256,454]{0,1:T(8,128)(4,1)S(1)} %fusion.41, bf16[256,20,64]{0,2,1:T(8,128)(2,1)} %bitcast.120, bf16[454,20,64]{0,2,1:T(8,128)(2,1)} %bitcast.118), kind=kOutput, calls=%fused_computation.95 | convolution fusion | flops 306831808 | bytes 11252224 | tf_op jit(solution)/shard_map/sub | solution.py:100
  135.6 6.1 %fusion.26 = bf16[20,64,256]{2,1,0:T(8,128)(2,1)} fusion(bf16[454,20,64]{0,2,1:T(8,128)(2,1)} %bitcast.119, f32[20,256,454]{1,2,0:T(8,128)} %get-tuple-element.16, f32[20,256]{1,0:T(8,128)S(1)} %get-tuple-element.15), kind=kOutput, calls=%fused_computation.39 | convolution fusion | flops 302510080 | bytes 11136000 | tf_op jit(solution)/shard_map/hqk,khd->qhd/dot_general | solution.py:102
  141.7 4.2 fusion.11
  145.8 2.1 reshape.244
  147.9 86.9 %all-gather.8.cloned.1.call-done = bf16[2560,2048]{1,0:T(8,128)(2,1)} async-done(((bf16[2560,128]{1,0:T(8,128)(2,1)}), bf16[2560,2048]{1,0:T(8,128)(2,1)}) %all-gather.8.cloned.1.call-update) | async-done | bytes 10485776 | tf_op jit(solution)/shard_map/all_gather | solution.py:113
  234.8 5.8 %multiply_reduce_fusion.1 = (f32[128]{0:T(128)S(1)}, f32[128,2048]{1,0:T(8,128)S(1)}) fusion(bf16[128,2560]{1,0:T(8,128)(2,1)} %reshape.244, bf16[2560,2048]{1,0:T(8,128)(2,1)} %all-gather.8.cloned.1.call-done), kind=kOutput, calls=%fused_computation.45 | convolution fusion | flops 1343225728 | bytes 12190208 | tf_op jit(solution)/shard_map/dot_general | solution.py:111
  240.6 0.0 copy-start.1
  240.6 1.1 convolution_convert_fusion.2
  241.7 0.0 copy-start.7
  241.7 82.5 %all_to_all.10 = bf16[16,48,2048]{2,1,0:T(8,128)(2,1)S(1)} all-to-all(bf16[16,48,2048]{2,1,0:T(8,128)(2,1)S(1)} %bitcast.117), channel_id=1, replica_groups=mesh['grp_0'=4,'grp_1'=4,'seq'=16] {'seq'}, dimensions={0} | all-to-all | bytes 6291456 | tf_op jit(solution)/shard_map/all_to_all | solution.py:136
  324.2 1.7 copy-done.3
  325.9 0.0 copy-done.7
  325.9 4.1 fusion.9
  330.0 10.9 %convolution_convert_fusion.1 = bf16[16,48,2048]{2,1,0:T(8,128)(2,1)} fusion(bf16[1,768,2048]{2,1,0:T(8,128)(2,1)S(1)} %copy-done, bf16[16,48,2048]{2,1,0:T(8,128)(2,1)} %copy-done.3, bf16[1,2048,768]{2,1,0:T(8,128)(2,1)} %param.20, f32[16,48,768]{2,1,0:T(8,128)} %fusion.9), kind=kOutput, calls=%fused_computation.12 | convolution fusion | flops 4836950016 | bytes 14942208 | tf_op jit(solution)/shard_map/secf,efd->secd/dot_general | solution.py:144
  340.9 4.8 %all-to-all-start.1 = ((bf16[16,48,2048]{2,1,0:T(8,128)(2,1)}), bf16[16,48,2048]{2,1,0:T(8,128)(2,1)}, u32[]{:S(2)}, u32[]{:S(2)}) async-start(bf16[16,48,2048]{2,1,0:T(8,128)(2,1)} %convolution_convert_fusion.1), calls=%async_computation.1 | async-start | bytes 6291456 | tf_op jit(solution)/shard_map/all_to_all | solution.py:146
  345.7 0.1 mul.97
  345.8 0.0 copy-done.5
  345.8 0.1 copy.29
  346.0 69.2 %all-to-all-done.1 = bf16[16,48,2048]{2,1,0:T(8,128)(2,1)} async-done(((bf16[16,48,2048]{2,1,0:T(8,128)(2,1)}), bf16[16,48,2048]{2,1,0:T(8,128)(2,1)}, u32[]{:S(2)}, u32[]{:S(2)}) %all-to-all-start.1) | async-done | bytes 3145760 | tf_op jit(solution)/shard_map/all_to_all | solution.py:146
  415.1 7.5 %gather_fusion = bf16[512,2048]{1,0:T(8,128)(2,1)} fusion(bf16[768,2048]{1,0:T(8,128)(2,1)} %bitcast.26, s32[1024]{0:T(1024)S(1)} %pad_clamp_fusion), kind=kCustom, calls=%fused_computation | custom fusion | bytes 4196352 | tf_op jit(solution)/shard_map/gather | solution.py:149
  422.7 4.8 %reshape.252 = f32[128,4,2048]{2,1,0:T(4,128)} reshape(bf16[512,2048]{1,0:T(8,128)(2,1)} %gather_fusion) | data formatting | bytes 6291456 | tf_op jit(solution)/shard_map/convert_element_type | solution.py:149
  427.4 5.5 %multiply_reduce_fusion = f32[128,2048]{1,0:T(8,128)S(1)} fusion(f32[128,4,2048]{2,1,0:T(4,128)} %reshape.252, f32[128,4]{1,0:T(8,128)S(1)} %copy.29), kind=kLoop, calls=%fused_computation.11 | loop fusion | flops 1835008 | bytes 5244928 | tf_op jit(solution)/shard_map/reduce_sum | solution.py:153
  433.0 0.9 fusion.38
  (26 shorter events, 0.2 us)
Async XLA Ops:
  6.5 323.5 %copy-start = (bf16[1,768,2048]{2,1,0:T(8,128)(2,1)S(1)}, bf16[1,768,2048]{2,1,0:T(8,128)(2,1)}, u32[]{:S(2)}) copy-start(bf16[1,768,2048]{2,1,0:T(8,128)(2,1)} %param.21) | copy-start | bytes 9437188
  6.5 89.2 %copy-start.8 = (f32[1280]{0:T(1024)S(1)}, f32[1280]{0:T(1024)}, u32[]{:S(2)}) copy-start(f32[1280]{0:T(1024)} %param.14) | copy-start | bytes 15364
  6.5 89.2 %all-gather.4.cloned.1.call-start = ((), (), s32[]{:S(2)}) async-start(), calls=%async_computation.2 | async-start | bytes 10444800 | tf_op jit(solution)/shard_map/all_gather | solution.py:75
  7.3 134.4 %all-gather.6.cloned.1.call-start = ((), (), s32[]{:S(2)}) async-start(), calls=%async_computation.3 | async-start | bytes 4096000 | tf_op jit(solution)/shard_map/all_gather | solution.py:36
  21.7 213.1 %all-gather.8.cloned.1.call-start = ((), (), s32[]{:S(2)}) async-start(), calls=%async_computation.4 | async-start | bytes 11141120 | tf_op jit(solution)/shard_map/all_gather | solution.py:113
  23.2 86.6 %collective-permute-start.2 = (bf16[99]{0:T(256)(128)(2,1)S(1)}, bf16[99]{0:T(256)(128)(2,1)S(1)}, u32[]{:S(2)}, u32[]{:S(2)}) collective-permute-start(bf16[99]{0:T(256)(128)(2,1)S(1)} %get-tuple-element.13), channel_id=1, source_target_pairs={{0,1},{1,2},{2,3},{3,4},{4,5},{5,6},{6,7},{7,8},{8,9},{9,10},{10,1... | collective-permute-start | bytes 602 | tf_op jit(solution)/shard_map/ppermute | solution.py:24
  30.1 79.7 %collective-permute-start.3 = (bf16[99]{0:T(256)(128)(2,1)S(1)}, bf16[99]{0:T(256)(128)(2,1)S(1)}, u32[]{:S(2)}, u32[]{:S(2)}) collective-permute-start(bf16[99]{0:T(256)(128)(2,1)S(1)} %get-tuple-element.14), channel_id=1, source_target_pairs={{1,0},{2,1},{3,2},{4,3},{5,4},{6,5},{7,6},{8,7},{9,8},{10,9},{11,1... | collective-permute-start | bytes 602 | tf_op jit(solution)/shard_map/ppermute | solution.py:26
  37.7 72.1 %copy-start.6 = (s32[1,256]{1,0:T(1,128)S(1)}, s32[1,256]{1,0:T(1,128)}, u32[]{:S(2)}) copy-start(s32[1,256]{1,0:T(1,128)} %param.13) | copy-start | bytes 3076
  103.7 10.6 %collective-permute-start = (bf16[99,2560]{1,0:T(8,128)(2,1)}, bf16[99,2560]{1,0:T(8,128)(2,1)}, u32[]{:S(2)}, u32[]{:S(2)}) collective-permute-start(bf16[99,2560]{1,0:T(8,128)(2,1)} %get-tuple-element.9), channel_id=1, source_target_pairs={{0,1},{1,2},{2,3},{3,4},{4,5},{5,6},{6,7},{7,8},{8,9},{9,10},{10,1... | collective-permute-start | bytes 1520648 | tf_op jit(solution)/shard_map/ppermute | solution.py:24
  107.6 11.2 %collective-permute-start.1 = (bf16[99,2560]{1,0:T(8,128)(2,1)}, bf16[99,2560]{1,0:T(8,128)(2,1)}, u32[]{:S(2)}, u32[]{:S(2)}) collective-permute-start(bf16[99,2560]{1,0:T(8,128)(2,1)} %get-tuple-element.10), channel_id=1, source_target_pairs={{1,0},{2,1},{3,2},{4,3},{5,4},{6,5},{7,6},{8,7},{9,8},{10,9},{11,1... | collective-permute-start | bytes 1520648 | tf_op jit(solution)/shard_map/ppermute | solution.py:26
  147.9 92.7 %copy-start.4 = (f32[2048]{0:T(1024)S(1)}, f32[2048]{0:T(1024)}, u32[]{:S(2)}) copy-start(f32[2048]{0:T(1024)} %param.18) | copy-start | bytes 24580
  240.6 83.6 %copy-start.1 = (f32[128,2048]{1,0:T(8,128)}, f32[128,2048]{1,0:T(8,128)S(1)}, u32[]{:S(2)}) copy-start(f32[128,2048]{1,0:T(8,128)S(1)} %get-tuple-element.18) | copy-start | bytes 3145732
  241.7 84.2 %copy-start.7 = (bf16[1,2048,768]{2,1,0:T(8,128)(2,1)S(1)}, bf16[1,2048,768]{2,1,0:T(8,128)(2,1)}, u32[]{:S(2)}) copy-start(bf16[1,2048,768]{2,1,0:T(8,128)(2,1)} %param.19) | copy-start | bytes 9437188
  324.2 1.7 copy-start.3
  340.9 4.9 %copy-start.5 = (f32[1,128,4]{1,2,0:T(4,128)S(1)}, f32[1,128,4]{1,2,0:T(4,128)}, u32[]{:S(2)}) copy-start(f32[1,128,4]{1,2,0:T(4,128)} %param.23) | copy-start | bytes 6148
  340.9 74.2 %all-to-all-start.1 = ((bf16[16,48,2048]{2,1,0:T(8,128)(2,1)}), bf16[16,48,2048]{2,1,0:T(8,128)(2,1)}, u32[]{:S(2)}, u32[]{:S(2)}) async-start(bf16[16,48,2048]{2,1,0:T(8,128)(2,1)} %convolution_convert_fusion.1), calls=%async_computation.1 | async-start | bytes 6291456 | tf_op jit(solution)/shard_map/all_to_all | solution.py:146
  427.4 5.5 %copy-start.2 = (f32[128,2048]{1,0:T(8,128)S(1)}, f32[128,2048]{1,0:T(8,128)}, u32[]{:S(2)}) copy-start(f32[128,2048]{1,0:T(8,128)} %copy-done.1) | copy-start | bytes 3145732
Sparse Core Ops, SparseCore 0:
  9.8 85.9 all-gather.3
  97.6 42.8 all-gather.5
  142.9 91.8 all-gather.7
where the time goes:
time: 441 us; the launch traced here: 440 us
  waiting for transfers between devices  220 us (50%)
  blocking collectives  96.8 us (22%)
  matrix products  47.2 us (11%)
  local copies, waits for them, and re-layouts  29.6 us (7%)
  starting transfers between devices  19.7 us (4%)
  other arithmetic  13.7 us (3%)
  between operations  13.4 us (3%)
    all_gather x1, waiting for transfers between devices, body(): lax.all_gather(adapter_weight, GRP, axis=1, tiled=True)  86.9 us
    all_to_all x1, blocking collectives, body(): lax.all_to_all(outgoing, 'seq', split_axis=0, concat_axis=0, tiled=True)  82.5 us
    all_to_all x1, waiting for transfers between devices, body(): lax.all_to_all(produced, 'seq', split_axis=0, concat_axis=0, tiled=True)  69.2 us
    all_gather x1, waiting for transfers between devices, body(): lax.all_gather(qkv_weight, GRP, axis=1, tiled=True)  58.1 us
    all_gather x1, blocking collectives, gather_axes(): out = lax.all_gather(out, axes[number], axis=dim, tiled=True)  14.3 us
    dot_general x1, matrix products, body(): jnp.einsum('secf,efd->secd', hidden, down_weight, preferred_element_type=...  10.9 us
    ppermute x2, starting transfers between devices, extended(): lax.ppermute(tail, axis, [(i, (i + 1) % count) for i in range(ends)])  10.8 us
  transfers between devices with their start and end apart: 8, of which 4 were waited for; matrix products, arithmetic and copies ran while one was open for 11% of the time, Pallas kernels for 0%

commit v1 on v0

--- a/solution.py
+++ b/solution.py
@@ -11,6 +11,11 @@
 LN_EPSILON = 1e-05
 RMS_EPSILON = 1e-06
 MASKED = -1e30
+
+
+def swapped_in(x, axis, dim):
+    sent = jnp.stack([x] * lax.axis_size(axis))
+    return jnp.concatenate(lax.all_to_all(sent, axis, 0, 0), axis=dim)
 
 
 def extended(cells, sides, width):
@@ -71,9 +76,7 @@
     signal = audio[0]
     normed = layer_norm(signal, norm_gain).astype(jnp.bfloat16)
     qkv_all = jnp.dot(
-        normed,
-        lax.all_gather(qkv_weight, GRP, axis=1, tiled=True),
-        preferred_element_type=jnp.float32,
+        normed, swapped_in(qkv_weight, GRP, 1), preferred_element_type=jnp.float32
     ).astype(jnp.bfloat16)
     tags = (block_ids[0] % 256 + 1).astype(jnp.float32).astype(jnp.bfloat16)
     key_value = qkv_all[:, width:]

time: 441 us -> 479 us (1.086)
  waiting for transfers between devices: 220 us -> 243 us
  starting transfers between devices: 19.7 us -> 29.7 us
    all_to_all x0 -> x1, waiting for transfers between devices: none -> 123 us  [swapped_in(): return jnp.concatenate(lax.all_to_all(sent, axis, 0, 0), axis=dim)]
    all_gather x1 -> x0, waiting for transfers between devices: 58.1 us -> none  [body(): lax.all_gather(qkv_weight, GRP, axis=1, tiled=True)]
    all_gather x1, waiting for transfers between devices: 86.9 us -> 48.3 us  [body(): lax.all_gather(adapter_weight, GRP, axis=1, tiled=True)]
    ppermute x2, starting transfers between devices: 4.02 us -> 12.4 us  [extended(): lax.ppermute(head, axis, [((i + 1) % count, i) for i in range(ends)])]
    another operation x1 -> x2, local copies, waits for them, and re-layouts: 0.01 us -> 5.44 us  [the longest x1 5.43 us: swapped_in(): sent = jnp.stack([x] * lax.axis_size(axis))]
    all_to_all x0 -> x1, starting transfers between devices: none -> 5.38 us  [swapped_in(): return jnp.concatenate(lax.all_to_all(sent, axis, 0, 0), axis=dim)]
  transfers between devices with their start and end apart: 8 -> 8, of which waited for: 4 -> 5; matrix products, arithmetic and copies ran while one was open for 11% -> 11% of each run, Pallas kernels for 0% -> 0%
where the time goes in v1:
time: 479 us; the launch traced here: 478 us
  waiting for transfers between devices  243 us (51%)
  blocking collectives  97 us (20%)
  matrix products  47.1 us (10%)
  local copies, waits for them, and re-layouts  34.3 us (7%)
  starting transfers between devices  29.7 us (6%)
  between operations  13.7 us (3%)
  other arithmetic  13.1 us (3%)
    all_to_all x1, waiting for transfers between devices, swapped_in(): return jnp.concatenate(lax.all_to_all(sent, axis, 0, 0), axis=dim)  123 us
    all_to_all x1, blocking collectives, body(): lax.all_to_all(outgoing, 'seq', split_axis=0, concat_axis=0, tiled=True)  82.5 us
    all_to_all x1, waiting for transfers between devices, body(): lax.all_to_all(produced, 'seq', split_axis=0, concat_axis=0, tiled=True)  69.2 us
    all_gather x1, waiting for transfers between devices, body(): lax.all_gather(adapter_weight, GRP, axis=1, tiled=True)  48.3 us
    all_gather x1, blocking collectives, gather_axes(): out = lax.all_gather(out, axes[number], axis=dim, tiled=True)  14.5 us
    ppermute x2, starting transfers between devices, extended(): lax.ppermute(head, axis, [((i + 1) % count, i) for i in range(ends)])  12.4 us
    dot_general x1, matrix products, body(): jnp.einsum('secf,efd->secd', hidden, down_weight, preferred_element_type=...  11 us
  transfers between devices with their start and end apart: 8, of which 5 were waited for; matrix products, arithmetic and copies ran while one was open for 11% of the time, Pallas kernels for 0%

profile of v1, /device:TPU:1, one launch (start us, length us, event | category | flops | bytes accessed | tf_op | source)
XLA Modules:
  0.0 478.1 jit_solution(8492060302653065535)
XLA Ops:
  6.5 0.0 copy-start
  6.5 0.0 all-gather.3.cloned.1.call-start
  6.5 14.5 %all_gather.9 = bf16[1280,320]{0,1:T(8,128)(2,1)} all-gather(bf16[1280,80]{0,1:T(8,128)(2,1)} %param.16), channel_id=1, replica_groups=mesh['grp_0'=4,'grp_1'=4,'seq'=16] {'grp_1'}, dimensions={1}, use_global_device_ids=true | all-gather | bytes 1024000 | tf_op jit(solution)/shard_map/all_gather | solution.py:41
  21.0 0.0 all-gather.3.cloned.1.call-update
  21.1 0.0 all-gather.5.cloned.1.call-start
  21.1 0.7 all-gather.5.cloned.1.call-update
  21.8 5.4 %stack.2 = bf16[16,1280,240]{1,2,0:T(8,128)(2,1)} broadcast(bf16[1280,240]{0,1:T(8,128)(2,1)} %param.15), dimensions={1,2} | broadcast | bytes 10444800 | tf_op jit(solution)/shard_map/stack | solution.py:17
  27.3 5.4 %all-to-all-start = ((bf16[16,1280,240]{1,2,0:T(8,128)(2,1)}), bf16[16,1280,240]{1,2,0:T(8,128)(2,1)}, u32[]{:S(2)}, u32[]{:S(2)}) async-start(bf16[16,1280,240]{1,2,0:T(8,128)(2,1)} %stack.2), calls=%async_computation | async-start | bytes 19660800 | tf_op jit(solution)/shard_map/all_to_all | solution.py:18
  32.6 0.0 copy-done.7
  32.7 0.1 fusion.62
  32.7 5.8 %collective-permute-start.3 = (bf16[99]{0:T(256)(128)(2,1)S(1)}, bf16[99]{0:T(256)(128)(2,1)S(1)}, u32[]{:S(2)}, u32[]{:S(2)}) collective-permute-start(bf16[99]{0:T(256)(128)(2,1)S(1)} %get-tuple-element.14), channel_id=1, source_target_pairs={{1,0},{2,1},{3,2},{4,3},{5,4},{6,5},{7,6},{8,7},{9,8},{10,9},{11,1... | collective-permute-start | bytes 602 | tf_op jit(solution)/shard_map/ppermute | solution.py:31
  38.6 3.4 collective-permute-start.2
  42.0 0.0 copy-done.6
  42.0 0.1 copy.31
  42.1 0.1 eq.62
  42.2 0.1 eq.66
  42.4 1.2 reduce-window.6
  43.5 0.2 slice_reduce_fusion
  43.8 0.1 fusion.44
  43.9 0.1 reduce_sum.72
  44.0 0.1 copy.35
  44.1 0.2 fusion.20
  44.3 1.3 convert_reduce_fusion
  45.6 1.4 fusion.26
  47.0 123.3 %all-to-all-done = bf16[16,1280,240]{1,2,0:T(8,128)(2,1)} async-done(((bf16[16,1280,240]{1,2,0:T(8,128)(2,1)}), bf16[16,1280,240]{1,2,0:T(8,128)(2,1)}, u32[]{:S(2)}, u32[]{:S(2)}) %all-to-all-start) | async-done | bytes 9830432 | tf_op jit(solution)/shard_map/all_to_all | solution.py:18
  170.3 0.0 copy-done.9
  170.3 6.8 %convolution_convert_fusion = bf16[256,3840]{1,0:T(8,128)(2,1)S(1)} fusion(bf16[1280,3840]{0,1:T(8,128)(2,1)} %bitcast.3, bf16[1,256,1280]{2,1,0:T(8,128)(2,1)} %param.12, f32[1280]{0:T(1024)S(1)} %copy-done.9, f32[256]{0:T(256)S(1)} %add_rsqrt_fusion, f32[256]{0:T(256)S(1)} %broadcast_multiply_fusion.1), kind=kOutput, calls=%fused_computation.6 | convolution fusion | flops 2519203840 | bytes 12459008 | tf_op jit(solution)/shard_map/dot_general | solution.py:78
  177.1 1.1 fusion.61
  178.2 6.6 %collective-permute-start.1 = (bf16[99,2560]{1,0:T(8,128)(2,1)}, bf16[99,2560]{1,0:T(8,128)(2,1)}, u32[]{:S(2)}, u32[]{:S(2)}) collective-permute-start(bf16[99,2560]{1,0:T(8,128)(2,1)} %get-tuple-element.10), channel_id=1, source_target_pairs={{1,0},{2,1},{3,2},{4,3},{5,4},{6,5},{7,6},{8,7},{9,8},{10,9},{11,1... | collective-permute-start | bytes 1520648 | tf_op jit(solution)/shard_map/ppermute | solution.py:31
  184.9 3.6 collective-permute-start
  188.5 0.0 collective-permute-done.3
  188.5 0.0 collective-permute-done.2
  188.6 0.1 maximum_convert_fusion
  188.6 0.2 fusion.42
  188.8 1.2 slice.45
  190.0 0.9 slice.48
  190.8 2.2 copy.28
  193.0 0.6 collective-permute-done.1
  193.6 1.2 collective-permute-done
  194.8 2.1 pad_maximum_fusion
  197.0 1.6 fusion.60
  198.5 2.4 copy.27
  200.9 2.4 copy.29
  203.3 8.2 %fusion.63 = (f32[20,256]{1,0:T(8,128)S(1)}, f32[20,256,454]{1,2,0:T(8,128)}) fusion(pred[256,454]{0,1:T(8,128)(4,1)S(1)} %fusion.42, bf16[256,20,64]{0,2,1:T(8,128)(2,1)} %bitcast.119, bf16[454,20,64]{0,2,1:T(8,128)(2,1)} %bitcast.118), kind=kOutput, calls=%fused_computation.97 | convolution fusion | flops 306831808 | bytes 11252224 | tf_op jit(solution)/shard_map/sub | solution.py:103
  211.5 6.0 %fusion.24 = bf16[20,64,256]{2,1,0:T(8,128)(2,1)} fusion(bf16[454,20,64]{0,2,1:T(8,128)(2,1)} %bitcast.117, f32[20,256,454]{1,2,0:T(8,128)} %get-tuple-element.16, f32[20,256]{1,0:T(8,128)S(1)} %get-tuple-element.15), kind=kOutput, calls=%fused_computation.38 | convolution fusion | flops 302510080 | bytes 11136000 | tf_op jit(solution)/shard_map/hqk,khd->qhd/dot_general | solution.py:105
  217.6 4.2 fusion.11
  221.8 2.1 reshape.275
  223.9 48.3 %all-gather.5.cloned.1.call-done = bf16[2560,2048]{1,0:T(8,128)(2,1)} async-done(((bf16[2560,128]{1,0:T(8,128)(2,1)}), bf16[2560,2048]{1,0:T(8,128)(2,1)}) %all-gather.5.cloned.1.call-update) | async-done | bytes 10485776 | tf_op jit(solution)/shard_map/all_gather | solution.py:116
  272.2 5.8 %multiply_reduce_fusion.1 = (f32[128]{0:T(128)S(1)}, f32[128,2048]{1,0:T(8,128)S(1)}) fusion(bf16[128,2560]{1,0:T(8,128)(2,1)} %reshape.275, bf16[2560,2048]{1,0:T(8,128)(2,1)} %all-gather.5.cloned.1.call-done), kind=kOutput, calls=%fused_computation.46 | convolution fusion | flops 1343225728 | bytes 12190208 | tf_op jit(solution)/shard_map/dot_general | solution.py:114
  278.0 1.1 convolution_convert_fusion.2
  279.1 0.0 copy-start.8
  279.1 82.5 %all_to_all.15 = bf16[16,48,2048]{2,1,0:T(8,128)(2,1)S(1)} all-to-all(bf16[16,48,2048]{2,1,0:T(8,128)(2,1)S(1)} %bitcast.116), channel_id=1, replica_groups=mesh['grp_0'=4,'grp_1'=4,'seq'=16] {'seq'}, dimensions={0} | all-to-all | bytes 6291456 | tf_op jit(solution)/shard_map/all_to_all | solution.py:139
  361.6 1.7 copy-done.3
  363.3 4.0 fusion.9
  367.3 11.0 %convolution_convert_fusion.1 = bf16[16,48,2048]{2,1,0:T(8,128)(2,1)} fusion(bf16[1,768,2048]{2,1,0:T(8,128)(2,1)S(1)} %copy-done, bf16[16,48,2048]{2,1,0:T(8,128)(2,1)} %copy-done.3, bf16[1,2048,768]{2,1,0:T(8,128)(2,1)} %param.20, f32[16,48,768]{2,1,0:T(8,128)} %fusion.9), kind=kOutput, calls=%fused_computation.12 | convolution fusion | flops 4836950016 | bytes 14942208 | tf_op jit(solution)/shard_map/secf,efd->secd/dot_general | solution.py:147
  378.3 4.8 all-to-all-start.2
  383.1 0.1 mul.99
  383.2 0.0 copy-done.5
  383.2 0.1 copy.30
  383.4 69.2 %all-to-all-done.2 = bf16[16,48,2048]{2,1,0:T(8,128)(2,1)} async-done(((bf16[16,48,2048]{2,1,0:T(8,128)(2,1)}), bf16[16,48,2048]{2,1,0:T(8,128)(2,1)}, u32[]{:S(2)}, u32[]{:S(2)}) %all-to-all-start.2) | async-done | bytes 3145760 | tf_op jit(solution)/shard_map/all_to_all | solution.py:149
  452.6 7.5 %gather_fusion = bf16[512,2048]{1,0:T(8,128)(2,1)} fusion(bf16[768,2048]{1,0:T(8,128)(2,1)} %bitcast.29, s32[1024]{0:T(1024)S(1)} %pad_clamp_fusion), kind=kCustom, calls=%fused_computation | custom fusion | bytes 4196352 | tf_op jit(solution)/shard_map/gather | solution.py:152
  460.1 4.8 reshape.283
  464.8 5.5 %multiply_reduce_fusion = f32[128,2048]{1,0:T(8,128)S(1)} fusion(f32[128,4,2048]{2,1,0:T(4,128)} %reshape.283, f32[128,4]{1,0:T(8,128)S(1)} %copy.30), kind=kLoop, calls=%fused_computation.11 | loop fusion | flops 1835008 | bytes 5244928 | tf_op jit(solution)/shard_map/reduce_sum | solution.py:156
  470.3 0.9 fusion.39
  (28 shorter events, 0.2 us)
Async XLA Ops:
  6.5 360.8 %copy-start = (bf16[1,768,2048]{2,1,0:T(8,128)(2,1)S(1)}, bf16[1,768,2048]{2,1,0:T(8,128)(2,1)}, u32[]{:S(2)}) copy-start(bf16[1,768,2048]{2,1,0:T(8,128)(2,1)} %param.21) | copy-start | bytes 9437188
  6.5 211.0 %all-gather.3.cloned.1.call-start = ((), (), s32[]{:S(2)}) async-start(), calls=%async_computation.3 | async-start | bytes 4096000 | tf_op jit(solution)/shard_map/all_gather | solution.py:41
  21.1 251.1 %all-gather.5.cloned.1.call-start = ((), (), s32[]{:S(2)}) async-start(), calls=%async_computation.4 | async-start | bytes 11141120 | tf_op jit(solution)/shard_map/all_gather | solution.py:116
  27.2 5.4 %copy-start.7 = (s32[1,256]{1,0:T(1,128)S(1)}, s32[1,256]{1,0:T(1,128)}, u32[]{:S(2)}) copy-start(s32[1,256]{1,0:T(1,128)} %param.13) | copy-start | bytes 3076
  27.2 14.8 %copy-start.6 = (s32[1,128,4]{1,2,0:T(4,128)S(1)}, s32[1,128,4]{1,2,0:T(4,128)}, u32[]{:S(2)}) copy-start(s32[1,128,4]{1,2,0:T(4,128)} %param.22) | copy-start | bytes 6148
  27.3 143.0 %copy-start.9 = (f32[1280]{0:T(1024)S(1)}, f32[1280]{0:T(1024)}, u32[]{:S(2)}) copy-start(f32[1280]{0:T(1024)} %param.14) | copy-start | bytes 15364
  27.3 143.0 %all-to-all-start = ((bf16[16,1280,240]{1,2,0:T(8,128)(2,1)}), bf16[16,1280,240]{1,2,0:T(8,128)(2,1)}, u32[]{:S(2)}, u32[]{:S(2)}) async-start(bf16[16,1280,240]{1,2,0:T(8,128)(2,1)} %stack.2), calls=%async_computation | async-start | bytes 19660800 | tf_op jit(solution)/shard_map/all_to_all | solution.py:18
  32.7 155.8 %collective-permute-start.3 = (bf16[99]{0:T(256)(128)(2,1)S(1)}, bf16[99]{0:T(256)(128)(2,1)S(1)}, u32[]{:S(2)}, u32[]{:S(2)}) collective-permute-start(bf16[99]{0:T(256)(128)(2,1)S(1)} %get-tuple-element.14), channel_id=1, source_target_pairs={{1,0},{2,1},{3,2},{4,3},{5,4},{6,5},{7,6},{8,7},{9,8},{10,9},{11,1... | collective-permute-start | bytes 602 | tf_op jit(solution)/shard_map/ppermute | solution.py:31
  38.6 150.0 %collective-permute-start.2 = (bf16[99]{0:T(256)(128)(2,1)S(1)}, bf16[99]{0:T(256)(128)(2,1)S(1)}, u32[]{:S(2)}, u32[]{:S(2)}) collective-permute-start(bf16[99]{0:T(256)(128)(2,1)S(1)} %get-tuple-element.13), channel_id=1, source_target_pairs={{0,1},{1,2},{2,3},{3,4},{4,5},{5,6},{6,7},{7,8},{8,9},{9,10},{10,1... | collective-permute-start | bytes 602 | tf_op jit(solution)/shard_map/ppermute | solution.py:29
  178.2 15.4 %collective-permute-start.1 = (bf16[99,2560]{1,0:T(8,128)(2,1)}, bf16[99,2560]{1,0:T(8,128)(2,1)}, u32[]{:S(2)}, u32[]{:S(2)}) collective-permute-start(bf16[99,2560]{1,0:T(8,128)(2,1)} %get-tuple-element.10), channel_id=1, source_target_pairs={{1,0},{2,1},{3,2},{4,3},{5,4},{6,5},{7,6},{8,7},{9,8},{10,9},{11,1... | collective-permute-start | bytes 1520648 | tf_op jit(solution)/shard_map/ppermute | solution.py:31
  184.9 10.0 %collective-permute-start = (bf16[99,2560]{1,0:T(8,128)(2,1)}, bf16[99,2560]{1,0:T(8,128)(2,1)}, u32[]{:S(2)}, u32[]{:S(2)}) collective-permute-start(bf16[99,2560]{1,0:T(8,128)(2,1)} %get-tuple-element.9), channel_id=1, source_target_pairs={{0,1},{1,2},{2,3},{3,4},{4,5},{5,6},{6,7},{7,8},{8,9},{9,10},{10,1... | collective-permute-start | bytes 1520648 | tf_op jit(solution)/shard_map/ppermute | solution.py:29
  223.8 54.2 %copy-start.4 = (f32[2048]{0:T(1024)S(1)}, f32[2048]{0:T(1024)}, u32[]{:S(2)}) copy-start(f32[2048]{0:T(1024)} %param.18) | copy-start | bytes 24580
  278.0 83.6 %copy-start.1 = (f32[128,2048]{1,0:T(8,128)}, f32[128,2048]{1,0:T(8,128)S(1)}, u32[]{:S(2)}) copy-start(f32[128,2048]{1,0:T(8,128)S(1)} %get-tuple-element.18) | copy-start | bytes 3145732
  279.1 84.2 %copy-start.8 = (bf16[1,2048,768]{2,1,0:T(8,128)(2,1)S(1)}, bf16[1,2048,768]{2,1,0:T(8,128)(2,1)}, u32[]{:S(2)}) copy-start(bf16[1,2048,768]{2,1,0:T(8,128)(2,1)} %param.19) | copy-start | bytes 9437188
  361.6 1.7 copy-start.3
  378.3 4.9 %copy-start.5 = (f32[1,128,4]{1,2,0:T(4,128)S(1)}, f32[1,128,4]{1,2,0:T(4,128)}, u32[]{:S(2)}) copy-start(f32[1,128,4]{1,2,0:T(4,128)} %param.23) | copy-start | bytes 6148
  378.3 74.2 %all-to-all-start.2 = ((bf16[16,48,2048]{2,1,0:T(8,128)(2,1)}), bf16[16,48,2048]{2,1,0:T(8,128)(2,1)}, u32[]{:S(2)}, u32[]{:S(2)}) async-start(bf16[16,48,2048]{2,1,0:T(8,128)(2,1)} %convolution_convert_fusion.1), calls=%async_computation.2 | async-start | bytes 6291456 | tf_op jit(solution)/shard_map/all_to_all | solution.py:149
  464.8 5.5 %copy-start.2 = (f32[128,2048]{1,0:T(8,128)S(1)}, f32[128,2048]{1,0:T(8,128)}, u32[]{:S(2)}) copy-start(f32[128,2048]{1,0:T(8,128)} %copy-done.1) | copy-start | bytes 3145732
Sparse Core Ops, SparseCore 0:
  21.2 145.9 all-gather.2
  169.6 102.5 all-gather.4
